TPU v7x, 32 devices: a whole 2x2x4 slice. The times are simulated.
32 devices in a mesh: groups: 2 (over y), node: 4 (over z), rep: 4 (over x, core).
Axes of the slice: x: 2, y: 2, z: 4, core: 2. Of those that a mesh axis runs over, the one named last changes fastest.
Arguments:
- node_states: bfloat16 [8, 512, 512], P(('groups', 'rep'), 'node'), parts along dimension 0, may hold values from -6 to 6
- cotangent: bfloat16 [8, 512, 512], P(('groups', 'rep'), 'node'), parts along dimension 0, may hold values from -1.1953125 to 1.1953125
- reach_blocks: int32 [8, 8, 8], P(('groups', 'rep'), 'node'), parts along dimension 0, may hold values from 0 to 7, as said below
- reach_count: int32 [8, 8], P(('groups', 'rep'), 'node'), parts along dimension 0, may hold values from 1 to 8, as said below
- level_start: int32 [8, 17], P(('groups', 'rep')), parts along dimension 0, may hold values from 0 to 512, as said below
- query_weight: bfloat16 [512, 256], replicated, may hold values from -0.25 to 0.25
- key_weight: bfloat16 [512, 256], replicated, may hold values from -0.25 to 0.25
- value_weight: bfloat16 [512, 256], replicated, may hold values from -0.25 to 0.25
- out_weight: bfloat16 [256, 512], replicated, may hold values from -0.375 to 0.375
- bias_table: float32 [4, 32], replicated, may hold values from -4 to 412
Outputs:
- updated: bfloat16 [8, 512, 512], P(('groups', 'rep'), 'node'), parts along dimension 0
- node_state_gradient: bfloat16 [8, 512, 512], P(('groups', 'rep'), 'node'), parts along dimension 0
- grad_query: float32 [1024, 256], P('groups'), parts along dimension 0
- grad_key: float32 [1024, 256], P('groups'), parts along dimension 0
- grad_value: float32 [1024, 256], P('groups'), parts along dimension 0
- grad_out: float32 [512, 512], P('groups'), parts along dimension 0
There are 2 independent parts, one for each index of `groups`. A program takes and returns all parts, laid end to end along the dimension named above; an argument that names none is the same for every part. Nothing has to cross between parts.
Inputs may be any that keep to these rules, and one draw needn't show every extreme that they name: `reach_blocks`: in row b of a graph, entry 0 is b, entries 1 to min(b, 7) are distinct blocks below b, and any later entries are b. `reach_count`: row b holds at most b + 1; row 7 of every graph holds 8. `level_start`: strictly increasing; entry 0 is 0 and entry 16 is 512.
All inputs are finite; a program needn't handle non-finite values.
Results may differ from a plain program's by a relative error of at most 0.011.
Values may be sent and summed in bfloat16 or wider, within the bound.
No kernel may reach another device: no remote copies, remote signals or barrier semaphores. Data moves between devices by JAX's collectives and lax.ppermute only.
A program may use at most 64 MiB of HBM per device.

v0:
```python
import jax
import jax.numpy as jnp
from jax import lax
from jax.sharding import PartitionSpec as P

HEADS = 4
HEAD = 64
BLOCK = 64
DIST = 32
EPS = 1e-05
NEG = -1e30
HIGH = lax.Precision.HIGHEST
CONTRACT_ROWS = (((0,), (0,)), ((), ()))
CONTRACT_COLS = (((1,), (1,)), ((), ()))


def rows_product(left, right):
    return lax.dot_general(left, right, CONTRACT_ROWS, preferred_element_type=jnp.float32)


def cols_product(left, right):
    return lax.dot_general(left, right, CONTRACT_COLS, preferred_element_type=jnp.float32)


def expand(listed):
    return jnp.repeat(jnp.repeat(listed, BLOCK, axis=0), BLOCK, axis=1)


def level_tables(starts, total, bias_table):
    level_count = starts.shape[0] - 1
    places = jnp.arange(total, dtype=jnp.int32)
    inner = starts[1:level_count]
    levels = jnp.sum((places[:, None] >= inner[None, :]).astype(jnp.int32), axis=1)
    marks = jnp.arange(level_count, dtype=jnp.int32)
    onehot = (levels[:, None] == marks[None, :]).astype(jnp.float32)
    spread = jnp.clip(marks[:, None] - marks[None, :], 0, DIST - 1)
    picks = (spread[:, :, None] == jnp.arange(DIST, dtype=jnp.int32)[None, None, :]).astype(
        jnp.float32
    )
    level_bias = jnp.einsum("hd,abd->hab", bias_table, picks, precision=HIGH)
    return (levels, onehot, level_bias)


def bias_block(row_onehot, head_bias, col_onehot):
    row_part = jnp.dot(row_onehot, head_bias, precision=HIGH)
    return lax.dot_general(row_part, col_onehot, CONTRACT_COLS, precision=HIGH)


def on_device(
    node_states,
    cotangent,
    reach_blocks,
    reach_count,
    level_start,
    query_weight,
    key_weight,
    value_weight,
    out_weight,
    bias_table,
):
    states = node_states[0]
    grads_in = cotangent[0]
    blocks = reach_blocks[0]
    counts = reach_count[0]
    starts = level_start[0]
    rows_dev = states.shape[0]
    width = query_weight.shape[1]
    total = rows_dev * lax.axis_size("node")
    offset = lax.axis_index("node") * rows_dev
    scale = HEAD ** (-0.5)
    key_blocks = total // BLOCK
    states_single_float = states.astype(jnp.float32)
    inverse_norm_scale = lax.rsqrt(
        jnp.mean(states_single_float * states_single_float, axis=1, keepdims=True) + EPS
    )
    centered_states = states_single_float * inverse_norm_scale
    normalized_states = centered_states.astype(jnp.bfloat16)
    queries = jnp.dot(normalized_states, query_weight, preferred_element_type=jnp.float32).astype(
        jnp.bfloat16
    )
    keys = jnp.dot(normalized_states, key_weight, preferred_element_type=jnp.float32).astype(
        jnp.bfloat16
    )
    values = jnp.dot(normalized_states, value_weight, preferred_element_type=jnp.float32).astype(
        jnp.bfloat16
    )
    keys_all, values_all = (
        lax.all_gather(keys, "node", axis=0, tiled=True),
        lax.all_gather(values, "node", axis=0, tiled=True),
    )
    levels, onehot, level_bias = level_tables(starts, total, bias_table)
    positions = jnp.arange(total, dtype=jnp.int32)
    local = jnp.arange(rows_dev, dtype=jnp.int32)
    row_ids = offset + local
    row_levels = lax.dynamic_slice_in_dim(levels, offset, rows_dev, 0)
    row_onehot = lax.dynamic_slice_in_dim(onehot, offset, rows_dev, 0)
    slots = jnp.arange(blocks.shape[1], dtype=jnp.int32)
    live = slots[None, :] < counts[:, None]
    kinds = jnp.arange(key_blocks, dtype=jnp.int32)
    listed = jnp.any((blocks[:, :, None] == kinds[None, None, :]) & live[:, :, None], axis=1)
    visible = expand(listed) & (
        (levels[None, :] < row_levels[:, None]) | (positions[None, :] == row_ids[:, None])
    )
    prob_list = []
    lse_list = []
    mixed_list = []
    for head in range(HEADS):
        lower = head * HEAD
        scores = (
            cols_product(queries[:, lower : lower + HEAD], keys_all[:, lower : lower + HEAD])
            * scale
        )
        scores = scores + bias_block(row_onehot, level_bias[head], onehot)
        scores = jnp.where(visible, scores, NEG)
        peak = jnp.max(scores, axis=1, keepdims=True)
        mass = jnp.sum(jnp.where(visible, jnp.exp(scores - peak), 0.0), axis=1, keepdims=True)
        lse = peak + jnp.log(mass)
        probs = jnp.where(visible, jnp.exp(scores - lse), 0.0).astype(jnp.bfloat16)
        prob_list.append(probs)
        lse_list.append(lse)
        mixed_list.append(
            jnp.dot(probs, values_all[:, lower : lower + HEAD], preferred_element_type=jnp.float32)
        )
    mixed = jnp.concatenate(mixed_list, axis=1).astype(jnp.bfloat16)
    updated = (
        states_single_float + jnp.dot(mixed, out_weight, preferred_element_type=jnp.float32)
    ).astype(jnp.bfloat16)
    partial_out = rows_product(mixed, grads_in)
    d_mixed = cols_product(grads_in, out_weight).astype(jnp.bfloat16)
    score_grads = []
    delta_list = []
    query_grads = []
    for head in range(HEADS):
        lower = head * HEAD
        mixed_head = d_mixed[:, lower : lower + HEAD]
        delta = jnp.sum(
            mixed_head.astype(jnp.float32) * mixed[:, lower : lower + HEAD].astype(jnp.float32),
            axis=1,
            keepdims=True,
        )
        d_probs = cols_product(mixed_head, values_all[:, lower : lower + HEAD])
        d_scores = (prob_list[head].astype(jnp.float32) * (d_probs - delta)).astype(jnp.bfloat16)
        score_grads.append(d_scores)
        delta_list.append(delta)
        query_grads.append(
            jnp.dot(d_scores, keys_all[:, lower : lower + HEAD], preferred_element_type=jnp.float32)
            * scale
        )
    d_queries = jnp.concatenate(query_grads, axis=1).astype(jnp.bfloat16)
    key_pieces = []
    value_pieces = []
    for head in range(HEADS):
        lower = head * HEAD
        score_part = score_grads[head]
        prob_part = prob_list[head]
        key_pieces.append(rows_product(score_part, queries[:, lower : lower + HEAD]) * scale)
        value_pieces.append(rows_product(prob_part, d_mixed[:, lower : lower + HEAD]))
    key_value_grads = lax.psum_scatter(
        jnp.concatenate(key_pieces + value_pieces, axis=1).astype(jnp.bfloat16),
        "node",
        scatter_dimension=0,
        tiled=True,
    ).astype(jnp.float32)
    d_keys = key_value_grads[:, :width].astype(jnp.bfloat16)
    d_values = key_value_grads[:, width:].astype(jnp.bfloat16)
    normalized_gradient = (
        cols_product(d_queries, query_weight)
        + cols_product(d_keys, key_weight)
        + cols_product(d_values, value_weight)
    )
    node_state_gradient = (
        grads_in.astype(jnp.float32)
        + inverse_norm_scale
        * (
            normalized_gradient
            - centered_states
            * jnp.mean(normalized_gradient * centered_states, axis=1, keepdims=True)
        )
    ).astype(jnp.bfloat16)
    partial_query = rows_product(normalized_states, d_queries)
    partial_key = rows_product(normalized_states, d_keys)
    partial_value = rows_product(normalized_states, d_values)
    total_query, total_key, total_value, total_out = lax.psum(
        (partial_query, partial_key, partial_value, partial_out), ("node", "rep")
    )
    return (
        updated[None],
        node_state_gradient[None],
        total_query,
        total_key,
        total_value,
        total_out,
    )


def solution(mesh):
    in_specs = (
        P(("groups", "rep"), "node", None),
        P(("groups", "rep"), "node", None),
        P(("groups", "rep"), "node", None),
        P(("groups", "rep"), "node"),
        P(("groups", "rep"), None),
        P(),
        P(),
        P(),
        P(),
        P(),
    )
    out_specs = (
        P(("groups", "rep"), "node", None),
        P(("groups", "rep"), "node", None),
        P("groups", None),
        P("groups", None),
        P("groups", None),
        P("groups", None),
    )
    return jax.shard_map(
        on_device, mesh=mesh, in_specs=in_specs, out_specs=out_specs, check_vma=False
    )
```

profile of v0, /device:TPU:0, one launch (start us, length us, event | category | flops | bytes accessed | tf_op | source)
XLA Modules:
  0.0 189.7 jit_solution(12456625626089858018)
XLA Ops:
  7.3 0.6 copy-done.12
  8.0 0.7 copy-done.10
  8.9 0.6 copy-done.13
  9.5 1.0 fusion.42
  11.0 0.6 copy-done.11
  11.6 0.6 convolution_bitcast_fusion
  14.4 15.6 %all_gather.7 = bf16[512,256]{1,0:T(8,128)(2,1)S(1)} all-gather(bf16[128,256]{1,0:T(8,128)(2,1)S(1)} %convolution_convert_fusion.1), channel_id=1, replica_groups=mesh['groups'=2,'node'=4,'rep'=4] {'node'}, dimensions={0}, use_global_device_ids=true | all-gather | bytes 327680 | tf_op jit(solution)/shard_map/all_gather | solution.py:89
  30.0 14.6 %all_gather.6 = bf16[512,256]{1,0:T(8,128)(2,1)S(1)} all-gather(bf16[128,256]{1,0:T(8,128)(2,1)S(1)} %convolution_convert_fusion.2), channel_id=1, replica_groups=mesh['groups'=2,'node'=4,'rep'=4] {'node'}, dimensions={0}, use_global_device_ids=true | all-gather | bytes 327680 | tf_op jit(solution)/shard_map/all_gather | solution.py:88
  44.6 0.4 fusion.46
  45.0 0.4 fusion.43
  45.7 0.4 fusion.127
  46.0 0.4 fusion.44
  46.7 0.4 fusion.45
  47.1 0.4 fusion.125
  47.5 0.4 select_reduce_fusion.3
  49.0 0.4 copy-done.3
  52.7 1.0 copy.27
  55.0 1.0 fusion.50
  56.0 1.1 fusion.104
  57.1 19.4 %reduce-scatter.4.cloned.1.call-done = bf16[128,512]{1,0:T(8,128)(2,1)} async-done(((bf16[512,512]{1,0:T(8,128)(2,1)}), bf16[128,512]{1,0:T(8,128)(2,1)}) %reduce-scatter.4.cloned.1.call-update) | async-done | bytes 131088
  76.5 2.0 %fusion.78 = f32[512,256]{1,0:T(8,128)} fusion(bf16[128,512]{1,0:T(8,128)(2,1)} %reduce-scatter.4.cloned.1.call-done, bf16[1,128,512]{2,1,0:T(8,128)(2,1)S(1)} %copy-done.1, f32[128]{0:T(128)S(1)} %add_rsqrt_fusion), kind=kOutput, calls=%fused_computation.125 | convolution fusion | flops 33751040 | bytes 721408 | tf_op jit(solution)/shard_map/dot_general | solution.py:18
  78.5 1.1 fusion.75
  79.6 0.9 fusion.17
  80.7 0.3 fusion.37
  81.1 0.8 fusion.49
  81.9 95.8 %all-reduce.3.cloned.1.call-done = (f32[512,256]{1,0:T(8,128)}, f32[512,256]{1,0:T(8,128)}, f32[512,256]{1,0:T(8,128)}, f32[256,512]{1,0:T(8,128)}) async-done(((f32[512,256]{1,0:T(8,128)}, f32[512,256]{1,0:T(8,128)}, f32[512,256]{1,0:T(8,128)}, f32[256,512]{1,0:T(8,128)}), (f32[512,256]{1,0:T(8,128)}, f32[512,256]{1,0:T(8,128)}, f32[512,256]{1,0:T(8,128)}, ...) | async-done | bytes 2097168 | tf_op jit(solution)/shard_map/psum | solution.py:183
  177.7 1.9 %copy.53 = f32[512,256]{1,0:T(8,128)} copy(f32[512,256]{1,0:T(8,128)} %get-tuple-element.43) | data formatting | bytes 1048576
  179.6 0.8 copy.54
  180.4 0.4 copy-done.7
  180.8 0.8 copy.55
  181.6 0.4 copy-done.6
  182.0 0.8 copy.56
  (76 shorter events, 9.3 us)
Async XLA Ops:
  7.2 7.0 %copy-start = (bf16[512,256]{1,0:T(8,128)(2,1)S(1)}, bf16[512,256]{1,0:T(8,128)(2,1)}, u32[]{:S(2)}) copy-start(bf16[512,256]{1,0:T(8,128)(2,1)} %param.17) | copy-start | bytes 786436
  7.2 69.3 %reduce-scatter.4.cloned.1.call-start = ((), (), s32[]{:S(2)}) async-start(), calls=%async_computation.1 | async-start | bytes 655360
  7.3 0.7 copy-start.12
  8.0 0.7 copy-start.10
  8.8 0.7 copy-start.13
  10.9 0.7 copy-start.11
  11.6 1.7 copy-start.4
  12.3 1.0 copy-start.1
  12.9 1.0 copy-start.5
  48.5 1.0 copy-start.3
  48.7 0.9 copy-start.2
  53.7 123.9 %all-reduce.3.cloned.1.call-start = ((), (), s32[]{:S(2)}) async-start(), calls=%async_computation.2 | async-start | bytes 4194304 | tf_op jit(solution)/shard_map/psum | solution.py:183
  76.5 2.0 %copy-start.9 = (bf16[128,512]{1,0:T(8,128)(2,1)S(1)}, bf16[128,512]{1,0:T(8,128)(2,1)}, u32[]{:S(2)}) copy-start(bf16[128,512]{1,0:T(8,128)(2,1)} %reduce-scatter.4.cloned.1.call-done) | copy-start | bytes 393220
  177.6 1.9 %copy-start.8 = (f32[512,256]{1,0:T(8,128)S(1)}, f32[512,256]{1,0:T(8,128)}, u32[]{:S(2)}) copy-start(f32[512,256]{1,0:T(8,128)} %get-tuple-element.44) | copy-start | bytes 1572868
  179.6 1.2 copy-start.7
  180.8 1.2 copy-start.6
Sparse Core Ops, SparseCore 0:
  53.8 22.5 reduce-scatter.3
  81.0 96.5 all-reduce.2
where the time goes:
time: 190 us
  waiting for transfers between devices  115 us (61%)
  blocking collectives  30.2 us (16%)
  matrix products  16.7 us (9%)
  between operations  14.3 us (8%)
  local copies, waits for them, and re-layouts  10.3 us (5%)
  other arithmetic  2.95 us (2%)
    psum x1, waiting for transfers between devices, on_device(): lax.psum((partial_query, partial_key, partial_value, partial_out), ('node...  95.8 us
    unnamed x3, waiting for transfers between devices  19.4 us
    all_gather x1, blocking collectives, on_device(): lax.all_gather(values, 'node', axis=0, tiled=True)  15.6 us
    all_gather x1, blocking collectives, on_device(): lax.all_gather(keys, 'node', axis=0, tiled=True)  14.6 us
    unnamed x33, local copies, waits for them, and re-layouts  9.64 us
    dot_general x12, matrix products, rows_product(): lax.dot_general(left, right, CONTRACT_ROWS, preferred_element_type=jnp.fl...  6.81 us
  transfers between devices with their start and end apart: 2, of which 2 were waited for; matrix products, arithmetic and copies ran while one was open for 3% of the time, Pallas kernels for 0%

commit v1 on v0

--- a/solution.py
+++ b/solution.py
@@ -1,3 +1,4 @@
+import functools
 import jax
 import jax.numpy as jnp
 from jax import lax
@@ -12,6 +13,14 @@
 HIGH = lax.Precision.HIGHEST
 CONTRACT_ROWS = (((0,), (0,)), ((), ()))
 CONTRACT_COLS = (((1,), (1,)), ((), ()))
+
+
+def corner_check(raw, link_axis, named_axis):
+    arr_now = jax.lax.psum(jax.lax.psum(raw, axis_name=link_axis), named_axis)
+    return arr_now
+
+
+register_patches = functools.partial(corner_check, link_axis="rep", named_axis="node")
 
 
 def rows_product(left, right):
@@ -180,8 +189,8 @@
     partial_query = rows_product(normalized_states, d_queries)
     partial_key = rows_product(normalized_states, d_keys)
     partial_value = rows_product(normalized_states, d_values)
-    total_query, total_key, total_value, total_out = lax.psum(
-        (partial_query, partial_key, partial_value, partial_out), ("node", "rep")
+    total_query, total_key, total_value, total_out = register_patches(
+        (partial_query, partial_key, partial_value, partial_out)
     )
     return (
         updated[None],

time: 190 us -> 233 us (1.23)
  waiting for transfers between devices: 115 us -> 158 us
    psum x1 -> x2, waiting for transfers between devices: 95.8 us -> 139 us  [corner_check(): arr_now = jax.lax.psum(jax.lax.psum(raw, axis_name=link_axis), named_axis)]
    unnamed x3 -> x4, waiting for transfers between devices: 19.4 us -> 19.6 us
  transfers between devices with their start and end apart: 2 -> 3, of which waited for: 2 -> 3; matrix products, arithmetic and copies ran while one was open for 3% -> 2% of each run, Pallas kernels for 0% -> 0%
where the time goes in v1:
time: 233 us
  waiting for transfers between devices  158 us (68%)
  blocking collectives  30.2 us (13%)
  matrix products  16.7 us (7%)
  between operations  14.1 us (6%)
  local copies, waits for them, and re-layouts  10.3 us (4%)
  other arithmetic  2.96 us (1%)
    psum x2, waiting for transfers between devices, corner_check(): arr_now = jax.lax.psum(jax.lax.psum(raw, axis_name=link_axis), named_axis)  139 us
    unnamed x4, waiting for transfers between devices  19.6 us
    all_gather x1, blocking collectives, on_device(): lax.all_gather(values, 'node', axis=0, tiled=True)  15.6 us
    all_gather x1, blocking collectives, on_device(): lax.all_gather(keys, 'node', axis=0, tiled=True)  14.6 us
    unnamed x33, local copies, waits for them, and re-layouts  9.64 us
    dot_general x12, matrix products, rows_product(): lax.dot_general(left, right, CONTRACT_ROWS, preferred_element_type=jnp.fl...  6.82 us
  transfers between devices with their start and end apart: 3, of which 3 were waited for; matrix products, arithmetic and copies ran while one was open for 2% of the time, Pallas kernels for 0%

profile of v1, /device:TPU:0, one launch (start us, length us, event | category | flops | bytes accessed | tf_op | source)
XLA Modules:
  0.0 232.7 jit_solution(12442363032877997024)
XLA Ops:
  7.3 0.6 copy-done.12
  8.0 0.7 copy-done.10
  8.9 0.6 copy-done.13
  9.5 1.0 fusion.42
  11.0 0.6 copy-done.11
  11.6 0.6 convolution_bitcast_fusion
  14.4 15.6 %all_gather.7 = bf16[512,256]{1,0:T(8,128)(2,1)S(1)} all-gather(bf16[128,256]{1,0:T(8,128)(2,1)S(1)} %convolution_convert_fusion.1), channel_id=1, replica_groups=mesh['groups'=2,'node'=4,'rep'=4] {'node'}, dimensions={0}, use_global_device_ids=true | all-gather | bytes 327680 | tf_op jit(solution)/shard_map/all_gather | solution.py:98
  30.0 14.6 %all_gather.6 = bf16[512,256]{1,0:T(8,128)(2,1)S(1)} all-gather(bf16[128,256]{1,0:T(8,128)(2,1)S(1)} %convolution_convert_fusion.2), channel_id=1, replica_groups=mesh['groups'=2,'node'=4,'rep'=4] {'node'}, dimensions={0}, use_global_device_ids=true | all-gather | bytes 327680 | tf_op jit(solution)/shard_map/all_gather | solution.py:97
  44.6 0.4 fusion.46
  45.0 0.4 fusion.43
  45.7 0.4 fusion.127
  46.0 0.4 fusion.44
  46.7 0.4 fusion.45
  47.1 0.4 fusion.125
  47.5 0.4 select_reduce_fusion.3
  49.0 0.4 copy-done.3
  52.7 1.0 copy.27
  54.8 1.0 fusion.50
  55.8 1.1 fusion.104
  56.9 19.6 %reduce-scatter.4.cloned.1.call-done = bf16[128,512]{1,0:T(8,128)(2,1)} async-done(((bf16[512,512]{1,0:T(8,128)(2,1)}), bf16[128,512]{1,0:T(8,128)(2,1)}) %reduce-scatter.4.cloned.1.call-update) | async-done | bytes 131088
  76.5 2.0 fusion.78
  78.5 1.1 fusion.75
  79.7 50.3 %all-reduce.5.cloned.1.call-done = (f32[512,256]{1,0:T(8,128)}, f32[512,256]{1,0:T(8,128)}, f32[512,256]{1,0:T(8,128)}, f32[256,512]{1,0:T(8,128)}) async-done(((f32[512,256]{1,0:T(8,128)}, f32[512,256]{1,0:T(8,128)}, f32[512,256]{1,0:T(8,128)}, f32[256,512]{1,0:T(8,128)}), (f32[512,256]{1,0:T(8,128)}, f32[512,256]{1,0:T(8,128)}, f32[512,256]{1,0:T(8,128)}, ...) | async-done | bytes 2097168 | tf_op jit(solution)/shard_map/psum | solution.py:19
  130.0 0.9 fusion.17
  131.7 0.8 fusion.49
  132.5 88.4 %all-reduce.7.cloned.1.call-done = (f32[512,256]{1,0:T(8,128)}, f32[512,256]{1,0:T(8,128)}, f32[512,256]{1,0:T(8,128)}, f32[256,512]{1,0:T(8,128)}) async-done(((f32[512,256]{1,0:T(8,128)}, f32[512,256]{1,0:T(8,128)}, f32[512,256]{1,0:T(8,128)}, f32[256,512]{1,0:T(8,128)}), (f32[512,256]{1,0:T(8,128)}, f32[512,256]{1,0:T(8,128)}, f32[512,256]{1,0:T(8,128)}, ...) | async-done | bytes 2097168 | tf_op jit(solution)/shard_map/psum | solution.py:19
  220.9 1.9 copy.57
  222.9 0.8 copy.58
  223.7 0.4 copy-done.7
  224.1 0.8 copy.59
  224.9 0.4 copy-done.6
  225.3 0.8 copy.60
  (79 shorter events, 9.6 us)
Async XLA Ops:
  7.2 7.0 %copy-start = (bf16[512,256]{1,0:T(8,128)(2,1)S(1)}, bf16[512,256]{1,0:T(8,128)(2,1)}, u32[]{:S(2)}) copy-start(bf16[512,256]{1,0:T(8,128)(2,1)} %param.17) | copy-start | bytes 786436
  7.2 69.3 %reduce-scatter.4.cloned.1.call-start = ((), (), s32[]{:S(2)}) async-start(), calls=%async_computation.1 | async-start | bytes 655360
  7.3 0.7 copy-start.12
  8.0 0.7 copy-start.10
  8.8 0.7 copy-start.13
  10.9 0.7 copy-start.11
  11.6 1.7 copy-start.4
  12.3 1.0 copy-start.1
  12.9 1.0 copy-start.5
  48.5 1.0 copy-start.3
  48.7 0.9 copy-start.2
  53.7 76.3 %all-reduce.5.cloned.1.call-start = ((), (), s32[]{:S(2)}) async-start(), calls=%async_computation.2 | async-start | bytes 4194304 | tf_op jit(solution)/shard_map/psum | solution.py:19
  76.5 2.0 copy-start.9
  79.6 141.3 %all-reduce.7.cloned.1.call-start = ((), (), s32[]{:S(2)}) async-start(), calls=%async_computation.3 | async-start | bytes 4194304 | tf_op jit(solution)/shard_map/psum | solution.py:19
  220.9 1.9 copy-start.8
  222.9 1.2 copy-start.7
  224.1 1.2 copy-start.6
Sparse Core Ops, SparseCore 0:
  53.8 22.5 reduce-scatter.3
  79.8 50.2 all-reduce.4
  132.8 88.0 all-reduce.6
